TPU v7x, 32 devices: a whole 2x2x4 slice. The times are simulated.
32 devices in a mesh: seq: 16 (over z, x, core), head: 2 (over y).
Axes of the slice: x: 2, y: 2, z: 4, core: 2. Of those that a mesh axis runs over, the one named last changes fastest.
Arguments:
- queries: bfloat16 [4096, 4096], P('seq', 'head'), may hold values from -8 to 8
- keys: bfloat16 [4096, 4096], P('seq', 'head'), may hold values from -8 to 8
- values: bfloat16 [4096, 4096], P('seq', 'head'), may hold values from -6 to 6
- features: float32 [32, 128, 256], P('head'), may hold values from -6 to 6
- output_proj_weight: bfloat16 [4096, 4096], P('head', 'seq'), may hold values from -0.125 to 0.125
Outputs:
- mixed: bfloat16 [4096, 4096], P('seq', 'head')
All inputs are finite; a program needn't handle non-finite values.
Results may differ from a plain program's by a relative error of at most 0.005.
Values may be sent and summed in bfloat16 or wider, within the bound.
A program may use at most 192 MiB of HBM per device.

v0:
```python
import math

import jax
import jax.numpy as jnp
from jax import lax
from jax.sharding import PartitionSpec as P

DH = 128
M = 256


def entering(shard, axis, combine, identity):
    devices, here = (lax.axis_size(axis), lax.axis_index(axis))
    everything = jax.tree.map(lambda part: lax.all_gather(part, axis), shard)
    start = jax.tree.map(
        lambda part, zero: jnp.broadcast_to(jnp.asarray(zero, part.dtype), part.shape),
        shard,
        identity,
    )

    def turn(k, before):
        reached = k < here
        new = combine(before, jax.tree.map(lambda part: part[k], everything))
        return jax.tree.map(lambda a, b: jnp.where(reached, a, b), new, before)

    return lax.fori_loop(0, devices, turn, start)


def feature_map(x, direction):
    x = x * DH ** (-0.25)
    proj = jnp.einsum("htd,hdm->htm", x, direction, precision=lax.Precision.HIGHEST)
    return jnp.exp(proj - 0.5 * jnp.sum(x * x, axis=-1, keepdims=True)) / math.sqrt(M)


def add_states(earlier, later):
    return (earlier[0] + later[0], earlier[1] + later[1])


def shards(queries, keys, values, features, output_proj_weight):
    tok_rows = queries.shape[0]
    local_heads = features.shape[0]

    def split_heads(arr):
        return arr.astype(jnp.float32).reshape(tok_rows, local_heads, DH).transpose(1, 0, 2)

    query_random_feats = feature_map(split_heads(queries), features)
    key_random_feats = feature_map(split_heads(keys), features)
    value_heads = split_heads(values)
    current_state = jnp.einsum(
        "tck,tcp->tkp", key_random_feats, value_heads, precision=lax.Precision.HIGHEST
    )
    total_here = jnp.sum(key_random_feats, axis=1)
    zero_state = jnp.zeros_like(current_state)
    zero_total = jnp.zeros_like(total_here)
    prior_state, total_before = entering(
        (current_state, total_here), "seq", add_states, (zero_state, zero_total)
    )
    rows_idx = lax.broadcasted_iota(jnp.int32, (tok_rows, tok_rows), 0)
    cols_idx = lax.broadcasted_iota(jnp.int32, (tok_rows, tok_rows), 1)
    lower = (cols_idx <= rows_idx).astype(jnp.float32)
    causal_scores = (
        jnp.einsum(
            "htm,hsm->hts", query_random_feats, key_random_feats, precision=lax.Precision.HIGHEST
        )
        * lower
    )
    numer = jnp.einsum("hts,hsd->htd", causal_scores, value_heads, precision=lax.Precision.HIGHEST)
    numer = numer + jnp.einsum(
        "czk,ckn->czn", query_random_feats, prior_state, precision=lax.Precision.HIGHEST
    )
    denom = jnp.sum(causal_scores, axis=2) + jnp.einsum(
        "htm,hm->ht", query_random_feats, total_before, precision=lax.Precision.HIGHEST
    )
    attended = (
        (numer / denom[:, :, None])
        .transpose(1, 0, 2)
        .reshape(tok_rows, local_heads * DH)
        .astype(jnp.bfloat16)
    )
    width = output_proj_weight.shape[1] * lax.axis_size("seq") // lax.axis_size("head")
    partial_out = jnp.dot(
        attended,
        lax.all_gather(output_proj_weight, "seq", axis=1, tiled=True),
        preferred_element_type=jnp.float32,
    )
    summed = lax.psum(partial_out, "head")
    mine = lax.dynamic_slice_in_dim(summed, lax.axis_index("head") * width, width, 1)
    return mine.astype(jnp.bfloat16)


def solution(mesh):
    in_specs = (
        P("seq", "head"),
        P("seq", "head"),
        P("seq", "head"),
        P("head", None, None),
        P("head", "seq"),
    )
    out_specs = P("seq", "head")
    return jax.shard_map(shards, mesh=mesh, in_specs=in_specs, out_specs=out_specs, check_vma=False)
```

profile of v0, /device:TPU:26, one launch (start us, length us, event | category | flops | bytes accessed | tf_op | source)
XLA Modules:
  0.0 444.9 jit_solution(9893758930857570812)
XLA Ops:
  6.5 0.0 copy-start
  6.5 0.0 all-gather.7.cloned.1.call-start
  6.5 2.0 fusion.12
  8.5 0.0 copy-start.7
  8.5 1.9 fusion.9
  10.5 0.0 copy-done
  10.5 5.5 %fusion.5 = (f32[16,256]{1,0:T(8,128)S(1)}, f32[16,256,256]{2,1,0:T(8,128)S(1)}) fusion(f32[16,256]{1,0:T(8,128)S(1)} %get-tuple-element.154, f32[16,128,256]{2,1,0:T(8,128)S(1)} %copy-done, bf16[256,2048]{1,0:T(8,128)(2,1)} %param.8), kind=kOutput, calls=%fused_computation.10 | convolution fusion | flops 1614802944 | bytes 7372800 | tf_op jit(solution)/shard_map/htd,hdm->htm/dot_general | solution.py:31
  16.0 2.0 copy-done.5
  17.9 0.0 copy-done.7
  17.9 5.4 %fusion.6 = f32[16,256,128]{2,1,0:T(8,128)} fusion(f32[16,256,256]{2,1,0:T(8,128)S(1)} %get-tuple-element.151, f32[16,256]{1,0:T(8,128)S(1)} %get-tuple-element.154, bf16[256,2048]{1,0:T(8,128)(2,1)S(1)} %copy-done.7), kind=kOutput, calls=%fused_computation.11 | convolution fusion | flops 1612709888 | bytes 7356416 | tf_op jit(solution)/shard_map/tck,tcp->tkp/dot_general | solution.py:49
  23.3 0.0 all-gather.7.cloned.1.call-update
  23.3 0.0 all-gather.5.cloned.1.call-start
  23.4 0.7 all-gather.5.cloned.1.call-update
  24.1 1.2 copy.31
  25.3 18.2 %all-gather.1 = f32[256,256]{1,0:T(8,128)S(1)} all-gather(f32[16,256]{1,0:T(8,128)S(1)} %get-tuple-element.150), channel_id=3, replica_groups=mesh['seq'=16,'head'=2] {'seq'}, dimensions={0}, use_global_device_ids=true | all-gather | bytes 278528 | tf_op jit(solution)/shard_map/all_gather | solution.py:14
  43.5 4.9 %fusion.11 = f32[16,256,256]{2,1,0:T(8,128)S(1)} fusion(f32[16,128,256]{2,1,0:T(8,128)S(1)} %copy-done, bf16[256,2048]{1,0:T(8,128)(2,1)} %param.7), kind=kOutput, calls=%fused_computation.18 | convolution fusion | flops 1611661312 | bytes 7340032 | tf_op jit(solution)/shard_map/htd,hdm->htm/dot_general | solution.py:31
  48.5 2.0 copy-done.3
  50.5 0.0 copy-done.6
  50.5 7.0 %multiply_reduce_fusion = (f32[16,256]{1,0:T(8,128)S(1)}, f32[16,256,256]{1,2,0:T(8,128)}) fusion(f32[256,256]{0,1:T(8,128)S(1)} %fusion.30, f32[16,256,256]{2,1,0:T(8,128)S(1)} %copy-done.6, f32[16,256]{1,0:T(8,128)S(1)} %get-tuple-element.154, f32[16,256,256]{2,1,0:T(8,128)S(1)} %fusion.11, f32[16,256]{1,0:T(8,128)S(1)} %get-tuple-element.155), kind=kOutput, calls=%fused_computation.4 | convolution fusion | flops 3227512832 | bytes 12894208 | tf_op jit(solution)/shard_map/htm,hsm->hts/dot_general | solution.py:62
  57.5 135.5 %all-gather.7.cloned.1.call-done = f32[256,256,128]{2,1,0:T(8,128)} async-done(((f32[16,256,128]{2,1,0:T(8,128)}), f32[256,256,128]{2,1,0:T(8,128)}) %all-gather.7.cloned.1.call-update) | async-done | bytes 33554448 | tf_op jit(solution)/shard_map/all_gather | solution.py:14
  193.0 38.0 %while.16 = (s32[]{:T(128)}, f32[16,256,128]{2,1,0:T(8,128)S(1)}, f32[16,256]{1,0:T(8,128)S(1)}, s32[]{:T(128)}, f32[16,16,256,128]{3,2,1,0:T(8,128)}, /*index=5*/f32[16,16,256]{2,1,0:T(8,128)S(1)}, s32[]{:T(128)}, s32[]{:T(128)}) while((s32[]{:T(128)}, f32[16,256,128]{2,1,0:T(8,128)S(1)}, f32[16,256]{1,0:T(8,128)S(1)}, s32[]{:T(128)}, ...), condition=%wide.region_4.5_spmd.clone, body=%wide.region_3.4_spmd.clone.sunk | while | flops 1585156 | bytes 6340723 | solution.py:26
  193.0 2.3 add_select_fusion.4
  195.4 2.3 add_select_fusion.4
  197.7 2.3 add_select_fusion.4
  200.1 2.3 add_select_fusion.4
  202.4 2.5 add_select_fusion.4
  204.9 2.4 add_select_fusion.4
  207.4 2.4 add_select_fusion.4
  209.8 2.3 add_select_fusion.4
  212.2 2.3 add_select_fusion.4
  214.5 2.3 add_select_fusion.4
  216.9 2.3 add_select_fusion.4
  219.2 2.4 add_select_fusion.4
  221.6 2.3 add_select_fusion.4
  224.0 2.3 add_select_fusion.4
  226.4 2.3 add_select_fusion.4
  228.7 2.3 add_select_fusion.4
  231.1 0.0 copy-start.4
  231.1 6.6 %fusion.2 = f32[16,1,256]{2,1,0:T(1,128)S(1)} fusion(f32[16,256,256]{2,1,0:T(8,128)} %copy-done.3, f32[16,256]{1,0:T(8,128)S(1)} %get-tuple-element.155, f32[16,256,1]{1,0,2:T(8,128)S(1)} %bitcast.87), kind=kOutput, calls=%fused_computation.7 | convolution fusion | flops 14680064 | bytes 4243456 | tf_op jit(solution)/shard_map/htm,hm->ht/dot_general | solution.py:71
  237.7 0.0 copy-done.4
  237.7 0.0 copy-start.8
  237.7 0.0 copy-start.9
  237.7 5.1 %fusion.3 = f32[16,256,128]{1,2,0:T(8,128)S(1)} fusion(f32[16,256,128]{2,1,0:T(8,128)S(1)} %get-tuple-element.115, f32[16,256,256]{2,1,0:T(8,128)S(1)} %copy-done.4, f32[16,256]{1,0:T(8,128)S(1)} %get-tuple-element.155), kind=kOutput, calls=%fused_computation.8 | convolution fusion | flops 1612709888 | bytes 8404992 | tf_op jit(solution)/shard_map/czk,ckn->czn/dot_general | solution.py:68
  242.9 2.6 fusion.13
  245.4 79.1 %all-gather.5.cloned.1.call-done = bf16[2048,4096]{1,0:T(8,128)(2,1)} async-done(((bf16[2048,256]{1,0:T(8,128)(2,1)}), bf16[2048,4096]{1,0:T(8,128)(2,1)}) %all-gather.5.cloned.1.call-update) | async-done | bytes 16777232 | tf_op jit(solution)/shard_map/all_gather | solution.py:83
  324.5 10.3 %fusion.37 = f32[256,4096]{1,0:T(8,128)} fusion(bf16[256,2048]{0,1:T(8,128)(2,1)S(1)} %bitcast.85, bf16[2048,4096]{1,0:T(8,128)(2,1)} %all-gather.5.cloned.1.call-done), kind=kOutput, calls=%fused_computation.51 | convolution fusion | flops 4294967296 | bytes 22020096 | tf_op jit(solution)/shard_map/dot_general | solution.py:81
  334.8 101.0 %all-reduce.1 = bf16[256,4096]{1,0:T(8,128)(2,1)} all-reduce(f32[256,4096]{1,0:T(8,128)} %fusion.37), channel_id=1, replica_groups=mesh['seq'=16,'head'=2] {'head'}, use_global_device_ids=true, to_apply=%region_6.7 | all-reduce | flops 1048576 | bytes 6291456 | tf_op jit(solution)/shard_map/psum | solution.py:86
  435.8 2.3 dynamic-slice_convert_fusion
  (30 shorter events, 0.3 us)
Async XLA Ops:
  6.5 4.0 copy-start
  6.5 186.5 %all-gather.7.cloned.1.call-start = ((), (), s32[]{:S(2)}) async-start(), calls=%async_computation.1 | async-start | bytes 35651584 | tf_op jit(solution)/shard_map/all_gather | solution.py:14
  8.5 9.4 %copy-start.7 = (bf16[256,2048]{1,0:T(8,128)(2,1)S(1)}, bf16[256,2048]{1,0:T(8,128)(2,1)}, u32[]{:S(2)}) copy-start(bf16[256,2048]{1,0:T(8,128)(2,1)} %param.9) | copy-start | bytes 3145732
  16.0 2.0 copy-start.5
  23.3 301.2 %all-gather.5.cloned.1.call-start = ((), (), s32[]{:S(2)}) async-start(), calls=%async_computation | async-start | bytes 17825792 | tf_op jit(solution)/shard_map/all_gather | solution.py:83
  25.3 25.2 %copy-start.6 = (f32[16,256,256]{2,1,0:T(8,128)S(1)}, f32[16,256,256]{2,1,0:T(8,128)}, u32[]{:S(2)}) copy-start(f32[16,256,256]{2,1,0:T(8,128)} %copy-done.5) | copy-start | bytes 12582916
  48.4 2.0 copy-start.3
  50.5 142.5 %copy-start.2 = (f32[16,256,128]{2,1,0:T(8,128)S(1)}, f32[16,256,128]{2,1,0:T(8,128)}, u32[]{:S(2)}) copy-start(f32[16,256,128]{2,1,0:T(8,128)} %custom-call) | copy-start | bytes 6291460
  231.1 6.7 %copy-start.4 = (f32[16,256,256]{2,1,0:T(8,128)S(1)}, f32[16,256,256]{2,1,0:T(8,128)}, u32[]{:S(2)}) copy-start(f32[16,256,256]{2,1,0:T(8,128)} %copy-done.3) | copy-start | bytes 12582916
  237.7 5.1 %copy-start.8 = (f32[16,256,256]{1,2,0:T(8,128)S(1)}, f32[16,256,256]{1,2,0:T(8,128)}, u32[]{:S(2)}) copy-start(f32[16,256,256]{1,2,0:T(8,128)} %get-tuple-element.153) | copy-start | bytes 12582916
  237.7 5.1 %copy-start.9 = (bf16[32,8,16,128]{3,2,1,0:T(8,128)(2,1)S(1)}, bf16[32,8,16,128]{3,2,1,0:T(8,128)(2,1)}, u32[]{:S(2)}) copy-start(bf16[32,8,16,128]{3,2,1,0:T(8,128)(2,1)} %copy.31) | copy-start | bytes 3145732
  324.5 113.5 %copy-start.1 = (f32[16,128,256]{2,1,0:T(8,128)S(1)}, f32[16,128,256]{2,1,0:T(8,128)}, u32[]{:S(2)}) copy-start(f32[16,128,256]{2,1,0:T(8,128)} %param.10) | copy-start | bytes 6291460
Sparse Core Ops, SparseCore 0:
  23.4 169.5 all-gather.6
  195.2 129.3 all-gather.4
where the time goes:
time: 450 us; the launch traced here: 445 us
  waiting for transfers between devices  215 us (48%)
  blocking collectives  119 us (26%)
  matrix products  47.2 us (10%)
  other arithmetic  41.5 us (9%)
  between operations  13.6 us (3%)
  local copies, waits for them, and re-layouts  7.54 us (2%)
    all_gather x1, waiting for transfers between devices, entering(): everything = jax.tree.map(lambda part: lax.all_gather(part, axis), shard)  136 us
    psum x1, blocking collectives, shards(): summed = lax.psum(partial_out, 'head')  101 us
    all_gather x1, waiting for transfers between devices, shards(): lax.all_gather(output_proj_weight, 'seq', axis=1, tiled=True)  79.1 us
    select_n x32, other arithmetic, turn(): return jax.tree.map(lambda a, b: jnp.where(reached, a, b), new, before)  37.5 us
    all_gather x1, blocking collectives, entering(): everything = jax.tree.map(lambda part: lax.all_gather(part, axis), shard)  18.2 us
    dot_general x2, matrix products, feature_map(): jnp.einsum('htd,hdm->htm', x, direction, precision=lax.Precision.HIGHEST)  10.4 us
    dot_general x1, matrix products, shards(): jnp.dot(attended, lax.all_gather(output_proj_weight, 'seq', axis=1, tiled...  10.3 us
  transfers between devices with their start and end apart: 2, of which 2 were waited for; matrix products, arithmetic and copies ran while one was open for 15% of the time, Pallas kernels for 0%

commit v1 on v0

v1 whole, which is shorter than its diff:
```python
import math

import jax
import jax.numpy as jnp
from jax import lax
from jax.sharding import PartitionSpec as P

DH = 128
M = 256
HIGH = lax.Precision.HIGHEST


def feature_map(x, direction):
    x = x * DH ** (-0.25)
    proj = jnp.einsum("htd,hdm->htm", x, direction, precision=HIGH)
    return jnp.exp(proj - 0.5 * jnp.sum(x * x, axis=-1, keepdims=True)) / math.sqrt(M)


def shards(queries, keys, values, features, output_proj_weight):
    tok_rows = queries.shape[0]
    local_heads = features.shape[0]
    devices, here = lax.axis_size("seq"), lax.axis_index("seq")
    halves, half = lax.axis_size("head"), lax.axis_index("head")

    def split_heads(arr):
        return arr.astype(jnp.float32).reshape(tok_rows, local_heads, DH).transpose(1, 0, 2)

    kf = feature_map(split_heads(keys), features)
    v = split_heads(values)
    v = jnp.concatenate([v, jnp.ones((local_heads, tok_rows, 8), jnp.float32)], axis=2)
    state = jnp.einsum("htp,htk->hpk", v, kf, precision=HIGH)
    states = lax.all_gather(state.astype(jnp.bfloat16), "seq")
    state, weight = lax.optimization_barrier((state, output_proj_weight))
    whole = lax.all_gather(weight, "seq", axis=1, tiled=True)
    qf = feature_map(split_heads(queries), features)
    lower = jnp.tril(jnp.ones((tok_rows, tok_rows), jnp.float32))
    scores = jnp.einsum("htm,hsm->hts", qf, kf, precision=HIGH) * lower
    both = jnp.einsum("hts,hsd->htd", scores, v, precision=HIGH)
    earlier = (jnp.arange(devices) < here)[:, None, None, None]
    prior = jnp.sum(jnp.where(earlier, states.astype(jnp.float32), 0.0), axis=0)
    both = both + jnp.einsum("htk,hpk->htp", qf, prior, precision=HIGH)
    attended = both[:, :, :DH] / both[:, :, DH : DH + 1]
    attended = attended.transpose(1, 0, 2).reshape(tok_rows, local_heads * DH).astype(jnp.bfloat16)
    partial = jnp.dot(attended, whole, preferred_element_type=jnp.float32)
    width = partial.shape[1] // halves
    total = lax.dynamic_slice_in_dim(partial, half * width, width, 1)
    for shift in range(1, halves):
        theirs = lax.rem(half + shift, halves)
        piece = lax.dynamic_slice_in_dim(partial, theirs * width, width, 1).astype(jnp.bfloat16)
        got = lax.ppermute(piece, "head", [(i, (i + shift) % halves) for i in range(halves)])
        total = total + got.astype(jnp.float32)
    return total.astype(jnp.bfloat16)


def solution(mesh):
    in_specs = (
        P("seq", "head"),
        P("seq", "head"),
        P("seq", "head"),
        P("head", None, None),
        P("head", "seq"),
    )
    return jax.shard_map(
        shards, mesh=mesh, in_specs=in_specs, out_specs=P("seq", "head"), check_vma=False
    )
```

time: 450 us -> 299 us (0.66)
  blocking collectives: 119 us -> 0 us
  other arithmetic: 41.5 us -> 18.5 us
  matrix products: 47.2 us -> 40.9 us
    psum x1 -> x0, blocking collectives: 101 us -> none  [shards(): summed = lax.psum(partial_out, 'head')]
    select_n x32 -> x1, other arithmetic: 37.5 us -> 0.02 us  [shards(): lower = jnp.tril(jnp.ones((tok_rows, tok_rows), jnp.float32))]
    all_gather x2, waiting for transfers between devices: 215 us -> 189 us  [the longest x1 111 us: shards(): whole = lax.all_gather(weight, 'seq', axis=1, tiled=True)]
    ppermute x0 -> x1, waiting for transfers between devices: none -> 24.8 us  [shards(): lax.ppermute(piece, 'head', [(i, (i + shift) % halves) for i in range(hal...]
    all_gather x1 -> x0, blocking collectives: 18.2 us -> none  [entering(): everything = jax.tree.map(lambda part: lax.all_gather(part, axis), shard)]
    reduce_sum x0 -> x1, other arithmetic: none -> 11.4 us  [shards(): prior = jnp.sum(jnp.where(earlier, states.astype(jnp.float32), 0.0), axis=0)]
    dot_general x8 -> x7, matrix products: 47.2 us -> 40.9 us  [the longest x2 11.9 us: feature_map(): proj = jnp.einsum('htd,hdm->htm', x, direction, precision=HIGH)]
  transfers between devices with their start and end apart: 2 -> 3, of which waited for: 2 -> 3; matrix products, arithmetic and copies ran while one was open for 15% -> 11% of each run, Pallas kernels for 0% -> 0%
where the time goes in v1:
time: 299 us; the launch traced here: 295 us
  waiting for transfers between devices  214 us (72%)
  matrix products  40.9 us (14%)
  other arithmetic  18.5 us (6%)
  between operations  13.6 us (5%)
  local copies, waits for them, and re-layouts  6.51 us (2%)
    all_gather x1, waiting for transfers between devices, shards(): whole = lax.all_gather(weight, 'seq', axis=1, tiled=True)  111 us
    all_gather x1, waiting for transfers between devices, shards(): states = lax.all_gather(state.astype(jnp.bfloat16), 'seq')  77.5 us
    ppermute x1, waiting for transfers between devices, shards(): lax.ppermute(piece, 'head', [(i, (i + shift) % halves) for i in range(hal...  24.8 us
    dot_general x2, matrix products, feature_map(): proj = jnp.einsum('htd,hdm->htm', x, direction, precision=HIGH)  11.9 us
    reduce_sum x1, other arithmetic, shards(): prior = jnp.sum(jnp.where(earlier, states.astype(jnp.float32), 0.0), axis=0)  11.4 us
    dot_general x1, matrix products, shards(): partial = jnp.dot(attended, whole, preferred_element_type=jnp.float32)  8.28 us
    dot_general x1, matrix products, shards(): scores = jnp.einsum('htm,hsm->hts', qf, kf, precision=HIGH) * lower  6.97 us
  transfers between devices with their start and end apart: 3, of which 3 were waited for; matrix products, arithmetic and copies ran while one was open for 11% of the time, Pallas kernels for 0%

profile of v1, /device:TPU:26, one launch (start us, length us, event | category | flops | bytes accessed | tf_op | source)
XLA Modules:
  0.0 294.7 jit_solution(12855215793351295603)
XLA Ops:
  6.5 0.0 copy-start
  6.5 0.0 all-gather.6.cloned.1.call-start
  6.5 2.0 fusion.8
  8.5 0.0 copy-done
  8.5 7.0 %fusion.7 = f32[16,256,256]{2,1,0:T(8,128)} fusion(f32[16,128,256]{2,1,0:T(8,128)S(1)} %copy-done, bf16[256,2048]{1,0:T(8,128)(2,1)} %param.6), kind=kOutput, calls=%fused_computation.11 | convolution fusion | flops 1611661312 | bytes 7340032 | tf_op jit(solution)/shard_map/htd,hdm->htm/dot_general | solution.py:15
  15.5 1.5 copy.11
  17.0 5.6 %fusion.5 = bf16[16,136,256]{2,1,0:T(8,128)(2,1)} fusion(f32[16,256,256]{2,1,0:T(8,128)} %fusion.7, f32[16,256]{1,0:T(8,128)S(1)} %broadcast_multiply_fusion, bf16[16,256,128]{1,2,0:T(8,128)(2,1)S(1)} %bitcast.55), kind=kOutput, calls=%fused_computation.8 | convolution fusion | flops 1713373184 | bytes 6373376 | tf_op jit(solution)/shard_map/htp,htk->hpk/dot_general | solution.py:31
  22.6 0.0 all-gather.6.cloned.1.call-update
  22.6 0.0 all-gather.4.cloned.1.call-start
  22.6 0.7 all-gather.4.cloned.1.call-update
  23.4 0.0 copy-start.2
  23.4 2.0 fusion.11
  25.4 4.9 %fusion.10 = f32[16,256,256]{2,1,0:T(8,128)S(1)} fusion(f32[16,128,256]{2,1,0:T(8,128)S(1)} %copy-done, bf16[256,2048]{1,0:T(8,128)(2,1)} %param.5), kind=kOutput, calls=%fused_computation.15 | convolution fusion | flops 1611661312 | bytes 7340032 | tf_op jit(solution)/shard_map/htd,hdm->htm/dot_general | solution.py:15
  30.3 0.0 copy-start.3
  30.3 2.0 copy-done.3
  32.3 0.0 copy-done.2
  32.3 7.0 %fusion.4 = f32[16,256,256]{2,1,0:T(8,128)} fusion(f32[16,256,256]{2,1,0:T(8,128)S(1)} %fusion.10, f32[16,256,256]{2,1,0:T(8,128)S(1)} %copy-done.2, f32[16,256]{1,0:T(8,128)S(1)} %broadcast_multiply_fusion, f32[16,256]{1,0:T(8,128)S(1)} %broadcast_multiply_fusion.1), kind=kOutput, calls=%fused_computation.7 | convolution fusion | flops 3225419776 | bytes 12615680 | tf_op jit(solution)/shard_map/htm,hsm->hts/dot_general | solution.py:37
  39.3 77.5 %all-gather.6.cloned.1.call-done = bf16[256,136,256]{2,1,0:T(8,128)(2,1)} async-done(((bf16[16,136,256]{2,1,0:T(8,128)(2,1)}), bf16[256,136,256]{2,1,0:T(8,128)(2,1)}) %all-gather.6.cloned.1.call-update) | async-done | bytes 17825808 | tf_op jit(solution)/shard_map/all_gather | solution.py:32
  116.8 0.0 copy-start.4
  116.8 11.4 %fusion = f32[16,136,256]{2,1,0:T(8,128)S(1)} fusion(bf16[16,16,136,256]{3,2,1,0:T(8,128)(2,1)} %bitcast.54, pred[16]{0:T(512)(128)(4,1)S(1)} %iota_compare_fusion.1), kind=kLoop, calls=%fused_computation.1 | loop fusion | flops 26181632 | bytes 20054032 | tf_op jit(solution)/shard_map/reduce_sum | solution.py:40
  128.2 0.0 copy-done.4
  128.2 0.0 copy-start.5
  128.2 5.5 %fusion.3 = f32[16,256,136]{1,2,0:T(8,128)S(1)} fusion(f32[16,136,256]{2,1,0:T(8,128)S(1)} %fusion, f32[16,256,256]{2,1,0:T(8,128)S(1)} %copy-done.4, f32[16,256]{1,0:T(8,128)S(1)} %broadcast_multiply_fusion.1), kind=kOutput, calls=%fused_computation.6 | convolution fusion | flops 1713373184 | bytes 8667136 | tf_op jit(solution)/shard_map/htk,hpk->htp/dot_general | solution.py:41
  133.7 0.0 copy-done.5
  133.7 2.7 fusion.23
  136.5 0.2 fusion.12
  136.7 111.5 %all-gather.4.cloned.1.call-done = bf16[2048,4096]{1,0:T(8,128)(2,1)} async-done(((bf16[2048,256]{1,0:T(8,128)(2,1)}), bf16[2048,4096]{1,0:T(8,128)(2,1)}) %all-gather.4.cloned.1.call-update) | async-done | bytes 16777232 | tf_op jit(solution)/shard_map/all_gather | solution.py:34
  248.1 0.0 copy-start.1
  248.1 8.3 %fusion.34 = f32[256,4096]{1,0:T(8,128)S(1)} fusion(bf16[256,2048]{0,1:T(8,128)(2,1)S(1)} %bitcast.57, bf16[2048,4096]{1,0:T(8,128)(2,1)} %all-gather.4.cloned.1.call-done), kind=kOutput, calls=%fused_computation.47 | convolution fusion | flops 4294967296 | bytes 22020096 | tf_op jit(solution)/shard_map/dot_general | solution.py:44
  256.4 0.0 copy-start.6
  256.4 1.9 copy-done.6
  258.4 1.1 dynamic-slice_convert_fusion
  259.5 0.8 collective-permute-start
  260.2 24.8 %collective-permute-done = bf16[256,2048]{1,0:T(8,128)(2,1)S(1)} collective-permute-done((bf16[256,2048]{1,0:T(8,128)(2,1)}, bf16[256,2048]{1,0:T(8,128)(2,1)S(1)}, u32[]{:S(2)}, u32[]{:S(2)}) %collective-permute-start) | collective-permute-done | bytes 1048608 | tf_op jit(solution)/shard_map/ppermute | solution.py:50
  285.0 2.9 add_convert_fusion
  287.9 0.0 copy-done.1
  (6 shorter events, 0.0 us)
Async XLA Ops:
  6.5 2.0 copy-start
  6.5 110.2 %all-gather.6.cloned.1.call-start = ((), (), s32[]{:S(2)}) async-start(), calls=%async_computation.1 | async-start | bytes 18939904 | tf_op jit(solution)/shard_map/all_gather | solution.py:32
  22.6 225.6 %all-gather.4.cloned.1.call-start = ((), (), s32[]{:S(2)}) async-start(), calls=%async_computation | async-start | bytes 17825792 | tf_op jit(solution)/shard_map/all_gather | solution.py:34
  23.4 8.9 %copy-start.2 = (f32[16,256,256]{2,1,0:T(8,128)S(1)}, f32[16,256,256]{2,1,0:T(8,128)}, u32[]{:S(2)}) copy-start(f32[16,256,256]{2,1,0:T(8,128)} %fusion.7) | copy-start | bytes 12582916
  30.3 2.0 copy-start.3
  116.8 11.4 %copy-start.4 = (f32[16,256,256]{2,1,0:T(8,128)S(1)}, f32[16,256,256]{2,1,0:T(8,128)}, u32[]{:S(2)}) copy-start(f32[16,256,256]{2,1,0:T(8,128)} %copy-done.3) | copy-start | bytes 12582916
  128.2 5.5 %copy-start.5 = (f32[16,256,256]{2,1,0:T(8,128)S(1)}, f32[16,256,256]{2,1,0:T(8,128)}, u32[]{:S(2)}) copy-start(f32[16,256,256]{2,1,0:T(8,128)} %fusion.4) | copy-start | bytes 12582916
  248.1 39.7 %copy-start.1 = (f32[16,128,256]{2,1,0:T(8,128)S(1)}, f32[16,128,256]{2,1,0:T(8,128)}, u32[]{:S(2)}) copy-start(f32[16,128,256]{2,1,0:T(8,128)} %param.8) | copy-start | bytes 6291460
  256.4 1.9 copy-start.6
  259.5 25.5 %collective-permute-start = (bf16[256,2048]{1,0:T(8,128)(2,1)}, bf16[256,2048]{1,0:T(8,128)(2,1)S(1)}, u32[]{:S(2)}, u32[]{:S(2)}) collective-permute-start(bf16[256,2048]{1,0:T(8,128)(2,1)} %dynamic-slice_convert_fusion), channel_id=1, source_target_pairs={{0,1},{1,0},{2,3},{3,2},{4,5},{5,4},{6,7},{7,6},{8,9},{9,8},{10,11... | collective-permute-start | bytes 3145736 | tf_op jit(solution)/shard_map/ppermute | solution.py:50
Sparse Core Ops, SparseCore 0:
  22.7 94.0 all-gather.5
  118.9 129.1 all-gather.3

commit v2 on v1

--- a/solution.py
+++ b/solution.py
@@ -1,8 +1,11 @@
+import functools
 import math
 
 import jax
 import jax.numpy as jnp
 from jax import lax
+from jax.experimental import pallas as pl
+from jax.experimental.pallas import tpu as pltpu
 from jax.sharding import PartitionSpec as P
 
 DH = 128
@@ -16,7 +19,7 @@
     return jnp.exp(proj - 0.5 * jnp.sum(x * x, axis=-1, keepdims=True)) / math.sqrt(M)
 
 
-def shards(queries, keys, values, features, output_proj_weight):
+def plain(queries, keys, values, features, output_proj_weight):
     tok_rows = queries.shape[0]
     local_heads = features.shape[0]
     devices, here = lax.axis_size("seq"), lax.axis_index("seq")
@@ -52,6 +55,286 @@
     return total.astype(jnp.bfloat16)
 
 
+ROWS = DH + 8
+PLANE, DEPTH = 4, 4
+GROUPS = 4
+
+
+def kernel_body(heads, q_ref, k_ref, v_ref, f_ref, w_hbm, out_ref, wbuf, kf, qf, vt, both, state,
+                sib_state, below, xsend, xrecv, prior, back, att, acc, psend, precv,
+                load_sem, w_send, w_recv, s_send, s_recv, z_send, z_recv, x_send, x_recv,
+                b_send, b_recv, p_send, p_recv):
+    tok = q_ref.shape[0]
+    half_heads = heads // 2
+    per = half_heads // GROUPS
+    me, y = lax.axis_index("seq"), lax.axis_index("head")
+    n = lax.axis_size("seq")
+    z, x, c = me // PLANE, (me // 2) % 2, me % 2
+    sib, xn, up, down = me + 1 - 2 * c, me + 2 - 4 * x, me + PLANE, me - PLANE
+    has_up, has_down = z < DEPTH - 1, z > 0
+
+    load = pltpu.make_async_copy(w_hbm, wbuf.at[me], load_sem)
+    load.start()
+    barrier = pltpu.get_barrier_semaphore()
+
+    def greet(device):
+        pl.semaphore_signal(barrier, inc=1, device_id=device, device_id_type=pl.DeviceIdType.MESH)
+
+    greet((sib, y))
+    greet((xn, y))
+    greet((me, 1 - y))
+
+    @pl.when(has_up)
+    def _():
+        greet((up, y))
+
+    @pl.when(has_down)
+    def _():
+        greet((down, y))
+
+    pl.semaphore_wait(barrier, 3 + has_up.astype(jnp.int32) + has_down.astype(jnp.int32))
+
+    def remote(src, dst, ssem, rsem, device):
+        return pltpu.make_async_remote_copy(
+            src_ref=src, dst_ref=dst, send_sem=ssem, recv_sem=rsem, device_id=device,
+            device_id_type=pl.DeviceIdType.MESH)
+
+    started = []
+
+    def go(cond, copy):
+        if cond is None:
+            copy.start()
+        else:
+            pl.when(cond)(copy.start)
+        started.append((cond, copy))
+
+    def block(slot, way, device):
+        return remote(wbuf.at[slot], wbuf.at[slot], w_send.at[slot, way], w_recv.at[slot],
+                      (device, y))
+
+    def arrived(slot):
+        block(slot, 3, sib).wait_recv()
+
+    load.wait()
+    go(has_up, block(me, 0, up))
+    go(has_down, block(me, 1, down))
+    go(None, block(me, 2, xn))
+    go(None, block(me, 3, sib))
+
+    def both_ways(cond, *copies):
+        for one in copies:
+            go(cond, one)
+
+    def along(d):
+        above, under = me + PLANE * d, me - PLANE * d
+        ok = z >= d
+
+        @pl.when(ok)
+        def _():
+            arrived(under)
+        go(jnp.logical_and(ok, has_up), block(under, 0, up))
+        both_ways(ok, block(under, 2, xn), block(under, 3, sib))
+        ok = z + d < DEPTH
+
+        @pl.when(ok)
+        def _():
+            arrived(above)
+        go(jnp.logical_and(ok, has_down), block(above, 1, down))
+        both_ways(ok, block(above, 2, xn), block(above, 3, sib))
+
+    def across(d):
+        if d == 0:
+            arrived(xn)
+            go(None, block(xn, 3, sib))
+            return
+        for slot, ok in ((xn - PLANE * d, z >= d), (xn + PLANE * d, z + d < DEPTH)):
+            pl.when(ok)(functools.partial(arrived, slot))
+            go(ok, block(slot, 3, sib))
+
+    def head_cols(h):
+        return pl.ds(pl.multiple_of(h * DH, DH), DH)
+
+    def feature_map(ref, h):
+        t = ref[:, head_cols(h)].astype(jnp.float32) * DH ** (-0.25)
+        proj = jnp.dot(t, f_ref[h], precision=HIGH, preferred_element_type=jnp.float32)
+        return jnp.exp(proj - 0.5 * jnp.sum(t * t, axis=-1, keepdims=True)) * (1 / math.sqrt(M))
+
+    @pl.loop(0, heads)
+    def _(h):
+        kf[h] = feature_map(k_ref, h)
+        vt[h, :DH, :] = v_ref[:, head_cols(h)].astype(jnp.float32).T
+        vt[h, DH:, :] = jnp.ones((ROWS - DH, tok), jnp.float32)
+        state[h] = jnp.dot(vt[h], kf[h], precision=HIGH, preferred_element_type=jnp.float32)
+
+    mine, other = c * half_heads, (1 - c) * half_heads
+    swap = remote(state.at[pl.ds(other, half_heads)], sib_state, s_send, s_recv, (sib, y))
+    go(None, swap)
+    swap.wait_recv()
+
+    lower = (lax.broadcasted_iota(jnp.int32, (tok, tok), 1)
+             <= lax.broadcasted_iota(jnp.int32, (tok, tok), 0))
+
+    def transposed(a, b):
+        return lax.dot_general(a, b, (((1,), (1,)), ((), ())), precision=HIGH,
+                               preferred_element_type=jnp.float32)
+
+    def local_heads(start, count):
+        @pl.loop(start, start + count)
+        def _(h):
+            qf[h] = feature_map(q_ref, h)
+            scores = jnp.where(lower, transposed(qf[h], kf[h]), 0.0)
+            both[h] = transposed(scores, vt[h])
+
+    at_x0 = (x == 0).astype(jnp.float32)
+    for g in range(GROUPS):
+        part = pl.ds(g * per, per)
+        hop = remote(back.at[part], below.at[part], z_send.at[g], z_recv.at[g], (up, y))
+
+        @pl.when(has_down)
+        def _():
+            hop.wait_recv()
+
+        @pl.when(z == 0)
+        def _():
+            below[part] = jnp.zeros((per, ROWS, M), jnp.float32)
+
+        chip = state[pl.ds(mine + g * per, per)] + sib_state[part]
+        back[part] = below[part] + chip
+        xsend[part] = below[part] + at_x0 * chip
+        go(has_up, hop)
+        go(None, remote(xsend.at[part], xrecv.at[part], x_send.at[g], x_recv.at[g], (xn, y)))
+        local_heads(g * (heads // GROUPS), heads // GROUPS)
+        if g == 1:
+            along(1)
+            across(0)
+
+    at_c0, at_c1 = (c == 0).astype(jnp.float32), (c == 1).astype(jnp.float32)
+    for g in range(GROUPS):
+        part = pl.ds(g * per, per)
+        own = pl.ds(mine + g * per, per)
+        remote(xsend.at[part], xrecv.at[part], x_send.at[g], x_recv.at[g], (xn, y)).wait_recv()
+        base = below[part] + xrecv[part]
+        xrecv[part] = base + at_c0 * state[own]
+        prior[own] = base + at_c1 * sib_state[part]
+        go(None, remote(xrecv.at[part], prior.at[own], b_send.at[g], b_recv.at[g], (sib, y)))
+
+    def finish(start):
+        @pl.loop(0, half_heads)
+        def _(i):
+            h = start + i
+            total = both[h] + transposed(qf[h], prior[h])
+            att[:, head_cols(h)] = (total[:, :DH] / total[:, DH : DH + 1]).astype(att.dtype)
+
+    finish(mine)
+    along(2)
+    across(1)
+    for g in range(GROUPS):
+        theirs = pl.ds(other + g * per, per)
+        remote(xrecv.at[pl.ds(g * per, per)], prior.at[theirs], b_send.at[g], b_recv.at[g],
+               (sib, y)).wait_recv()
+    finish(other)
+
+    width = wbuf.shape[2]
+    halfn = n // 2
+
+    def out_copy(b):
+        i = b % halfn
+        return remote(psend.at[i], precv.at[i], p_send.at[i], p_recv.at[i], (me, 1 - y))
+
+    def bit(a, b):
+        return (a + b) % 2
+
+    def project(first, count):
+        @pl.loop(first, first + count)
+        def _(i):
+            b = ((bit(z // 2, i // 8) * 2 + bit(z % 2, (i // 4) % 2)) * PLANE
+                 + bit(x, (i // 2) % 2) * 2 + bit(c, i % 2))
+
+            @pl.when(i % 2 == 1)
+            def _():
+                arrived(b)
+            piece = jnp.dot(att[...], wbuf[b], preferred_element_type=jnp.float32)
+
+            @pl.when(b // halfn == y)
+            def _():
+                acc[b % halfn] = piece
+
+            @pl.when(b // halfn != y)
+            def _():
+                psend[b % halfn] = piece.astype(psend.dtype)
+                out_copy(b).start()
+
+    project(0, 2 * PLANE)
+    along(3)
+    across(2)
+    project(2 * PLANE, PLANE)
+    across(3)
+    project(3 * PLANE, PLANE)
+    for i in range(halfn):
+        out_copy(i).wait_recv()
+        out_ref[:, i * width : (i + 1) * width] = (
+            acc[i] + precv[i].astype(jnp.float32)).astype(out_ref.dtype)
+    for i in range(halfn):
+        out_copy(i).wait_send()
+    for cond, copy in started:
+        if cond is None:
+            copy.wait_send()
+        else:
+            pl.when(cond)(copy.wait_send)
+
+
+def fused(queries, keys, values, features, weight):
+    tok, columns = queries.shape
+    heads = features.shape[0]
+    n = lax.axis_size("seq")
+    depth, width = weight.shape
+    half = heads // 2
+    f32, bf16 = jnp.float32, jnp.bfloat16
+    vmem = pltpu.VMEM
+    dma = pltpu.SemaphoreType.DMA
+    inner = [pl.BlockSpec(memory_space=pltpu.VMEM)] * 4
+    return pl.pallas_call(
+        functools.partial(kernel_body, heads),
+        out_shape=jax.ShapeDtypeStruct((tok, width * n // 2), bf16),
+        in_specs=inner + [pl.BlockSpec(memory_space=pl.ANY)],
+        out_specs=pl.BlockSpec(memory_space=pltpu.VMEM),
+        scratch_shapes=[
+            vmem((n, depth, width), bf16),
+            vmem((heads, tok, M), f32),
+            vmem((heads, tok, M), f32),
+            vmem((heads, ROWS, tok), f32),
+            vmem((heads, tok, ROWS), f32),
+            vmem((heads, ROWS, M), f32),
+            vmem((half, ROWS, M), f32),
+            vmem((half, ROWS, M), f32),
+            vmem((half, ROWS, M), f32),
+            vmem((half, ROWS, M), f32),
+            vmem((heads, ROWS, M), f32),
+            vmem((half, ROWS, M), f32),
+            vmem((tok, columns), bf16),
+            vmem((n // 2, tok, width), f32),
+            vmem((n // 2, tok, width), bf16),
+            vmem((n // 2, tok, width), bf16),
+            dma, dma((n, 4)), dma((n,)), dma, dma,
+            dma((GROUPS,)), dma((GROUPS,)), dma((GROUPS,)), dma((GROUPS,)),
+            dma((GROUPS,)), dma((GROUPS,)), dma((n // 2,)), dma((n // 2,)),
+        ],
+        compiler_params=pltpu.CompilerParams(
+            collective_id=0, has_side_effects=True, vmem_limit_bytes=63 << 20),
+    )(queries, keys, values, features, weight)
+
+
+def shards(queries, keys, values, features, output_proj_weight):
+    fits = (
+        lax.axis_size("seq") == PLANE * DEPTH
+        and lax.axis_size("head") == 2
+        and features.shape[0] % (2 * GROUPS) == 0
+        and output_proj_weight.shape[1] % 128 == 0
+    )
+    step = fused if fits else plain
+    return step(queries, keys, values, features, output_proj_weight)
+
+
 def solution(mesh):
     in_specs = (
         P("seq", "head"),

time: 299 us -> 171 us (0.57); the launches traced: 295 us -> 170 us
  waiting for transfers between devices: 214 us -> 0 us
  Pallas kernels: 0 us -> 168 us
  matrix products: 40.9 us -> 0 us
  other arithmetic: 18.5 us -> 0 us
  between operations: 13.6 us -> 0.01 us
  local copies, waits for them, and re-layouts: 6.51 us -> 2.3 us
    all_gather x2 -> x0, waiting for transfers between devices: 189 us -> none  [the longest x1 111 us: shards(): whole = lax.all_gather(weight, 'seq', axis=1, tiled=True)]
    pallas_call x0 -> x1, Pallas kernels: none -> 168 us  [fused(): pl.pallas_call(functools.partial(kernel_body, heads), out_shape=jax.Shape...]
    dot_general x7 -> x0, matrix products: 40.9 us -> none  [the longest x2 11.9 us: feature_map(): proj = jnp.einsum('htd,hdm->htm', x, direction, precision=HIGH)]
    ppermute x1 -> x0, waiting for transfers between devices: 24.8 us -> none  [shards(): lax.ppermute(piece, 'head', [(i, (i + shift) % halves) for i in range(hal...]
    reduce_sum x3 -> x0, other arithmetic: 15.4 us -> none  [the longest x1 11.4 us: shards(): prior = jnp.sum(jnp.where(earlier, states.astype(jnp.float32), 0.0), axis=0)]
    unnamed x16 -> x1, local copies, waits for them, and re-layouts: 5.38 us -> 2.3 us
    convert_element_type x2 -> x0, other arithmetic: 3.07 us -> none  [the longest x1 2.85 us: shards(): return total.astype(jnp.bfloat16)]
  transfers between devices with their start and end apart: 3 -> 0, of which waited for: 3 -> 0; matrix products, arithmetic and copies ran while one was open for 11% -> 0% of each run, Pallas kernels for 0% -> 0%
where the time goes in v2:
time: 171 us; the launch traced here: 170 us
  Pallas kernels  168 us (98%)
  local copies, waits for them, and re-layouts  2.3 us (1%)
    pallas_call x1, Pallas kernels, fused(): pl.pallas_call(functools.partial(kernel_body, heads), out_shape=jax.Shape...  168 us

profile of v2, /device:TPU:26, one launch (start us, length us, event | category | flops | bytes accessed | tf_op | source)
XLA Modules:
  0.0 170.5 jit_solution(11610990823752449450)
XLA Ops:
  0.0 168.2 %shard_map.55 = bf16[256,2048]{1,0:T(8,128)(2,1)} custom-call(bf16[256,2048]{1,0:T(8,128)(2,1)} %q_ref.1, bf16[256,2048]{1,0:T(8,128)(2,1)} %k_ref.1, bf16[256,2048]{1,0:T(8,128)(2,1)} %v_ref.1, f32[16,128,256]{2,1,0:T(8,128)} %f_ref.1, bf16[2048,256]{1,0:T(8,128)(2,1)} %w_hbm.1), custom_call_target="tpu_custom_call" | custom-call | tf_op jit(solution)/shard_map/pallas_call | solution.py:296
  168.2 2.3 %copy.7 = bf16[256,2048]{1,0:T(8,128)(2,1)} copy(bf16[256,2048]{1,0:T(8,128)(2,1)} %shard_map.55) | data formatting | bytes 2097152

commit v3 on v2

--- a/solution.py
+++ b/solution.py
@@ -200,23 +200,25 @@
 
         chip = state[pl.ds(mine + g * per, per)] + sib_state[part]
         back[part] = below[part] + chip
-        xsend[part] = below[part] + at_x0 * chip
+        xsend[part] = (below[part] + at_x0 * chip).astype(xsend.dtype)
         go(has_up, hop)
         go(None, remote(xsend.at[part], xrecv.at[part], x_send.at[g], x_recv.at[g], (xn, y)))
         local_heads(g * (heads // GROUPS), heads // GROUPS)
         if g == 1:
             along(1)
-            across(0)
-
+
+    along(2)
+    across(0)
+    across(1)
     at_c0, at_c1 = (c == 0).astype(jnp.float32), (c == 1).astype(jnp.float32)
     for g in range(GROUPS):
         part = pl.ds(g * per, per)
         own = pl.ds(mine + g * per, per)
         remote(xsend.at[part], xrecv.at[part], x_send.at[g], x_recv.at[g], (xn, y)).wait_recv()
-        base = below[part] + xrecv[part]
-        xrecv[part] = base + at_c0 * state[own]
+        base = below[part] + xrecv[part].astype(jnp.float32)
+        below[part] = base + at_c0 * state[own]
         prior[own] = base + at_c1 * sib_state[part]
-        go(None, remote(xrecv.at[part], prior.at[own], b_send.at[g], b_recv.at[g], (sib, y)))
+        go(None, remote(below.at[part], prior.at[own], b_send.at[g], b_recv.at[g], (sib, y)))
 
     def finish(start):
         @pl.loop(0, half_heads)
@@ -226,13 +228,13 @@
             att[:, head_cols(h)] = (total[:, :DH] / total[:, DH : DH + 1]).astype(att.dtype)
 
     finish(mine)
-    along(2)
-    across(1)
+    along(3)
     for g in range(GROUPS):
         theirs = pl.ds(other + g * per, per)
-        remote(xrecv.at[pl.ds(g * per, per)], prior.at[theirs], b_send.at[g], b_recv.at[g],
+        remote(below.at[pl.ds(g * per, per)], prior.at[theirs], b_send.at[g], b_recv.at[g],
                (sib, y)).wait_recv()
     finish(other)
+    across(2)
 
     width = wbuf.shape[2]
     halfn = n // 2
@@ -264,10 +266,7 @@
                 psend[b % halfn] = piece.astype(psend.dtype)
                 out_copy(b).start()
 
-    project(0, 2 * PLANE)
-    along(3)
-    across(2)
-    project(2 * PLANE, PLANE)
+    project(0, 3 * PLANE)
     across(3)
     project(3 * PLANE, PLANE)
     for i in range(halfn):
@@ -307,8 +306,8 @@
             vmem((heads, ROWS, M), f32),
             vmem((half, ROWS, M), f32),
             vmem((half, ROWS, M), f32),
-            vmem((half, ROWS, M), f32),
-            vmem((half, ROWS, M), f32),
+            vmem((half, ROWS, M), bf16),
+            vmem((half, ROWS, M), bf16),
             vmem((heads, ROWS, M), f32),
             vmem((half, ROWS, M), f32),
             vmem((tok, columns), bf16),

time: 171 us -> 154 us (0.901)
  Pallas kernels: 168 us -> 151 us
    pallas_call x1, Pallas kernels: 168 us -> 151 us  [fused(): pl.pallas_call(functools.partial(kernel_body, heads), out_shape=jax.Shape...]
where the time goes in v3:
time: 154 us; the launch traced here: 153 us
  Pallas kernels  151 us (98%)
  local copies, waits for them, and re-layouts  2.3 us (1%)
    pallas_call x1, Pallas kernels, fused(): pl.pallas_call(functools.partial(kernel_body, heads), out_shape=jax.Shape...  151 us

profile of v3, /device:TPU:26, one launch (start us, length us, event | category | flops | bytes accessed | tf_op | source)
XLA Modules:
  0.0 153.4 jit_solution(8524840775143643799)
XLA Ops:
  0.0 151.1 %shard_map.55 = bf16[256,2048]{1,0:T(8,128)(2,1)} custom-call(bf16[256,2048]{1,0:T(8,128)(2,1)} %q_ref.1, bf16[256,2048]{1,0:T(8,128)(2,1)} %k_ref.1, bf16[256,2048]{1,0:T(8,128)(2,1)} %v_ref.1, f32[16,128,256]{2,1,0:T(8,128)} %f_ref.1, bf16[2048,256]{1,0:T(8,128)(2,1)} %w_hbm.1), custom_call_target="tpu_custom_call" | custom-call | tf_op jit(solution)/shard_map/pallas_call | solution.py:295
  151.1 2.3 %copy.7 = bf16[256,2048]{1,0:T(8,128)(2,1)} copy(bf16[256,2048]{1,0:T(8,128)(2,1)} %shard_map.55) | data formatting | bytes 2097152
